TPU v7x, 32 devices: a whole 2x2x4 slice. The times are simulated.
32 devices in a mesh: dp: 8 (over y, x, core), mp: 4 (over z).
Axes of the slice: x: 2, y: 2, z: 4, core: 2. Of those that a mesh axis runs over, the one named last changes fastest.
Arguments:
- patches: bfloat16 [1024, 6144], P('dp', 'mp'), may hold values from -64 to 64
- send_start: int32 [8, 8], P('dp'), may hold values from 0 to 128, as said below
- run_length: int32 [8, 8], P('dp'), may hold values from 0 to 32, as said below
- slot_start: int32 [8, 8], P('dp'), may hold values from 0 to 128, as said below
- image_ids: int32 [8, 128], P('dp'), may hold values from 0 to 7, never falling along the last dimension, each value on 1 to 32 neighbouring positions
- norm_gain: float32 [6144], replicated, may hold values from 0.1 to 1.9
- qkv_weight: bfloat16 [6144, 3, 4096], P('dp', None, 'mp'), may hold values from -0.078125 to 0.078125
- query_gain: float32 [128], replicated, may hold values from 0.1 to 1.9
- key_gain: float32 [128], replicated, may hold values from 0.1 to 1.9
- out_weight: bfloat16 [4096, 6144], P('mp'), may hold values from -0.09375 to 0.09375
Outputs:
- packed: bfloat16 [1024, 6144], P('dp', 'mp')
- attended: bfloat16 [1024, 6144], P('dp', 'mp')
Inputs may be any that keep to these rules, and one draw needn't show every extreme that they name: `run_length`: every source's runs sum to 128 and every pack's runs sum to 128; the longest run is exactly 32. `send_start`: the runs of one source device do not intersect and cover its 128 rows. `slot_start`: the runs into one pack do not intersect and fill its 128 slots. `image_ids`: image numbers never fall along a pack; equal numbers mark one image.
All inputs are finite; a program needn't handle non-finite values.
Results may differ from a plain program's by a relative error of at most 0.011.
Values may be sent and summed in bfloat16 or wider, within the bound.
A program may use at most 128 MiB of HBM per device.

v0:
```python
import jax
import jax.numpy as jnp
from jax import lax
from jax.sharding import PartitionSpec as P

epsilon = 1e-06


def row_norm(values, scales):
    middle = jnp.mean(values, axis=-1, keepdims=True)
    spread = jnp.mean(values * values, axis=-1, keepdims=True) - middle * middle
    return (values - middle) * lax.rsqrt(spread + epsilon) * scales


def on_device(
    patches,
    send_start,
    run_length,
    slot_start,
    image_ids,
    norm_gain,
    qkv_weight,
    query_gain,
    key_gain,
    out_weight,
):
    pack_rows, feat_local = patches.shape
    pack_count = lax.axis_size("dp")
    mp_count = lax.axis_size("mp")
    capacity = 2 * pack_rows // pack_count
    local_cols = qkv_weight.shape[1] * qkv_weight.shape[2]
    offsets = jnp.arange(capacity, dtype=jnp.int32)
    rows = jnp.arange(pack_rows, dtype=jnp.int32)
    x = patches.astype(jnp.float32)
    sums = jnp.stack([jnp.sum(x, axis=-1), jnp.sum(x * x, axis=-1)])
    sums = lax.psum(sums, "mp") / (feat_local * mp_count)
    middle = sums[0][:, None]
    spread = sums[1][:, None] - middle * middle
    gain = lax.dynamic_slice_in_dim(norm_gain, lax.axis_index("mp") * feat_local, feat_local)
    normed = ((x - middle) * lax.rsqrt(spread + epsilon) * gain).astype(jnp.bfloat16)
    wide = lax.all_gather(normed, "mp", axis=1, tiled=True)
    slices = lax.all_to_all(wide, "dp", split_axis=1, concat_axis=0, tiled=True)
    tables = jnp.concatenate([send_start, run_length, slot_start], axis=0)[None]
    tables = lax.all_gather(tables, "dp", axis=0, tiled=True)
    starts, lengths, slots = (tables[:, 0].T, tables[:, 1].T, tables[:, 2])
    inside = (rows >= slots[:, :, None]) & (rows < (slots + lengths)[:, :, None])
    base = jnp.arange(pack_count, dtype=jnp.int32)[None, :] * pack_rows + starts - slots
    origin = jnp.sum(jnp.where(inside, base[:, :, None] + rows, 0), axis=1).reshape(-1)
    chosen = (origin[:, None] == jnp.arange(origin.shape[0], dtype=jnp.int32)).astype(jnp.bfloat16)
    ordered = jnp.dot(chosen, slices, preferred_element_type=jnp.float32).astype(jnp.bfloat16)
    partial = jnp.dot(
        ordered,
        qkv_weight.reshape(qkv_weight.shape[0], local_cols),
        preferred_element_type=jnp.float32,
    ).astype(jnp.bfloat16)
    projected = lax.psum_scatter(partial, "dp", scatter_dimension=0, tiled=True).astype(jnp.float32)
    own_rows = send_start[0][:, None] + offsets[None, :]
    occupied = offsets[None, :] < run_length[0][:, None]
    pick = (occupied[:, :, None] & (own_rows[:, :, None] == rows)).astype(jnp.bfloat16)
    outgoing = jnp.dot(
        pick.reshape(-1, pack_rows), patches, preferred_element_type=jnp.float32
    ).astype(jnp.bfloat16)
    arrived = lax.all_to_all(
        outgoing.reshape(pack_count, capacity, feat_local),
        "dp",
        split_axis=0,
        concat_axis=0,
        tiled=True,
    )
    targets = (slot_start[0][:, None] + offsets[None, :]).reshape(-1)
    place = (rows[:, None] == targets[None, :]).astype(jnp.bfloat16)
    packed = jnp.dot(
        place, arrived.reshape(-1, feat_local), preferred_element_type=jnp.float32
    ).astype(jnp.bfloat16)
    head_size = query_gain.shape[0]
    heads_here = qkv_weight.shape[2] // head_size
    split_heads = projected.reshape(pack_rows, 3, heads_here, head_size)
    queries = row_norm(split_heads[:, 0], query_gain).astype(jnp.bfloat16)
    key_rows = row_norm(split_heads[:, 1], key_gain).astype(jnp.bfloat16)
    values = split_heads[:, 2].astype(jnp.bfloat16)
    scores = jnp.einsum(
        "qhd,khd->hqk", queries, key_rows, preferred_element_type=jnp.float32
    ) * head_size ** (-0.5)
    image_of = image_ids[0]
    same_image = image_of[:, None] == image_of[None, :]
    weights_raw = jnp.where(same_image[None], jnp.exp(scores), 0.0)
    totals = jnp.sum(weights_raw, axis=-1, keepdims=True)
    attention = (weights_raw / totals).astype(jnp.bfloat16)
    context = jnp.einsum(
        "hqk,khd->qhd", attention, values, preferred_element_type=jnp.float32
    ).astype(jnp.bfloat16)
    context = context.reshape(pack_rows, heads_here * head_size)
    partial_value = jnp.dot(context, out_weight, preferred_element_type=jnp.float32)
    attended = lax.psum_scatter(
        partial_value.astype(jnp.bfloat16), "mp", scatter_dimension=1, tiled=True
    )
    return (packed, attended)


def solution(mesh):
    return jax.shard_map(
        on_device,
        mesh=mesh,
        in_specs=(
            P("dp", "mp"),
            P("dp", None),
            P("dp", None),
            P("dp", None),
            P("dp", None),
            P(),
            P("dp", None, "mp"),
            P(),
            P(),
            P("mp", None),
        ),
        out_specs=(P("dp", "mp"), P("dp", "mp")),
        check_vma=False,
    )
```

profile of v0, /device:TPU:0, one launch (start us, length us, event | category | flops | bytes accessed | tf_op | source)
XLA Modules:
  0.0 220.3 jit_solution(4133471638652877734)
XLA Ops:
  7.2 1.2 copy.47
  8.4 0.2 convert_reduce_fusion
  8.7 13.5 %psum.7 = f32[2,128]{1,0:T(2,128)S(1)} all-reduce(f32[2,128]{1,0:T(2,128)S(1)} %pad_maximum_fusion), channel_id=1, replica_groups=mesh['dp'=8,'mp'=4] {'mp'}, use_global_device_ids=true, to_apply=%region_3.4 | all-reduce | flops 256 | bytes 2048 | tf_op jit(solution)/shard_map/psum | solution.py:36
  22.1 0.8 dynamic_slice.3
  22.9 1.0 fusion.8
  24.0 35.5 %all-gather.4.cloned.1.call-done = bf16[128,6144]{0,1:T(8,128)(2,1)} async-done(((bf16[128,1536]{0,1:T(8,128)(2,1)}), bf16[128,6144]{0,1:T(8,128)(2,1)}) %all-gather.4.cloned.1.call-update) | async-done | bytes 1572880 | tf_op jit(solution)/shard_map/all_gather | solution.py:41
  59.4 3.8 %all-to-all-start.1 = ((bf16[128,8,768]{0,2,1:T(8,128)(2,1)}), bf16[128,8,768]{0,2,1:T(8,128)(2,1)S(1)}, u32[]{:S(2)}, u32[]{:S(2)}) async-start(bf16[128,8,768]{0,2,1:T(8,128)(2,1)} %bitcast.83), calls=%async_computation.1 | async-start | bytes 3145728 | tf_op jit(solution)/shard_map/all_to_all | solution.py:42
  63.3 24.0 %all-gather.1 = s32[8,3,8]{2,1,0:T(4,128)S(1)} all-gather(s32[1,3,8]{2,1,0:T(4,128)S(1)} %add_bitcast_fusion), channel_id=2, replica_groups=mesh['dp'=8,'mp'=4] {'dp'}, dimensions={0}, use_global_device_ids=true | all-gather | bytes 864 | tf_op jit(solution)/shard_map/all_gather | solution.py:44
  87.5 6.7 %copy.49 = bf16[768,3,1024]{0,2,1:T(8,128)(2,1)} copy(bf16[768,3,1024]{2,0,1:T(8,128)(2,1)} %param.16) | data formatting | bytes 9437184 | tf_op args[6]
  94.2 0.1 select_reduce_fusion
  94.3 0.7 copy.48
  95.0 12.2 %convolution_convert_fusion.1 = bf16[1024,3072]{1,0:T(8,128)(2,1)} fusion(bf16[768,3072]{0,1:T(8,128)(2,1)} %bitcast.79, bf16[1024,768]{1,0:T(8,128)(2,1)S(1)} %bitcast.84, s32[1024]{0:T(1024)S(1)} %bitcast.91), kind=kOutput, calls=%fused_computation.1 | convolution fusion | flops 6447431680 | bytes 12587008 | tf_op jit(solution)/shard_map/dot_general | solution.py:51
  107.4 0.6 copy-done.1
  107.9 0.1 broadcast_compare_fusion
  108.0 59.1 %reduce-scatter.3.cloned.1.call-done = bf16[128,3072]{1,0:T(8,128)(2,1)} async-done(((bf16[1024,3072]{1,0:T(8,128)(2,1)}), bf16[128,3072]{1,0:T(8,128)(2,1)}) %reduce-scatter.3.cloned.1.call-update) | async-done | bytes 786448 | tf_op jit(solution)/shard_map/reduce_scatter | solution.py:56
  167.2 1.3 copy.58
  168.5 0.2 copy_convert_fusion
  168.7 0.3 slice_reduce_fusion.1
  169.0 0.3 fusion.16
  169.4 0.2 copy.57
  169.7 0.7 fusion.4
  170.4 0.3 convolution_convert_fusion.4
  170.7 7.6 %convolution_convert_fusion = bf16[128,6144]{1,0:T(8,128)(2,1)} fusion(bf16[128,1024]{0,1:T(8,128)(2,1)S(1)} %bitcast.86, bf16[1024,6144]{1,0:T(8,128)(2,1)} %param.19), kind=kOutput, calls=%fused_computation | convolution fusion | flops 1611399168 | bytes 14417920 | tf_op jit(solution)/shard_map/dot_general | solution.py:93
  178.4 0.1 add.117
  178.5 0.1 lt.37
  178.6 0.7 copy-done
  179.3 1.3 convolution_convert_fusion.2
  180.6 3.5 %all-to-all-start = ((bf16[8,32,1536]{2,1,0:T(8,128)(2,1)}), bf16[8,32,1536]{2,1,0:T(8,128)(2,1)S(1)}, u32[]{:S(2)}, u32[]{:S(2)}) async-start(bf16[8,32,1536]{2,1,0:T(8,128)(2,1)} %bitcast.3), calls=%async_computation | async-start | bytes 1572864 | tf_op jit(solution)/shard_map/all_to_all | solution.py:63
  184.2 0.1 add.111
  184.3 12.4 %all-to-all-done = bf16[8,32,1536]{2,1,0:T(8,128)(2,1)S(1)} async-done(((bf16[8,32,1536]{2,1,0:T(8,128)(2,1)}), bf16[8,32,1536]{2,1,0:T(8,128)(2,1)S(1)}, u32[]{:S(2)}, u32[]{:S(2)}) %all-to-all-start) | async-done | bytes 786464 | tf_op jit(solution)/shard_map/all_to_all | solution.py:63
  196.7 1.0 convolution_convert_fusion.3
  197.7 16.0 %reduce-scatter.5.cloned.1.call-done = bf16[128,1536]{1,0:T(8,128)(2,1)} async-done(((bf16[128,6144]{1,0:T(8,128)(2,1)}), bf16[128,1536]{1,0:T(8,128)(2,1)}) %reduce-scatter.5.cloned.1.call-update) | async-done | bytes 393232 | tf_op jit(solution)/shard_map/reduce_scatter | solution.py:94
  (34 shorter events, 0.6 us)
Async XLA Ops:
  7.2 52.3 %all-gather.4.cloned.1.call-start = ((), (), s32[]{:S(2)}) async-start(), calls=%async_computation.4 | async-start | bytes 1966080 | tf_op jit(solution)/shard_map/all_gather | solution.py:41
  59.4 3.8 %copy-start.2 = (s32[1,8]{1,0:T(1,128)S(1)}, s32[1,8]{1,0:T(1,128)}, u32[]{:S(2)}) copy-start(s32[1,8]{1,0:T(1,128)} %param.11) | copy-start | bytes 100
  59.4 3.8 %copy-start.3 = (s32[1,8]{1,0:T(1,128)S(1)}, s32[1,8]{1,0:T(1,128)}, u32[]{:S(2)}) copy-start(s32[1,8]{1,0:T(1,128)} %param.13) | copy-start | bytes 100
  59.4 3.9 %copy-start.4 = (s32[1,8]{1,0:T(1,128)S(1)}, s32[1,8]{1,0:T(1,128)}, u32[]{:S(2)}) copy-start(s32[1,8]{1,0:T(1,128)} %param.12) | copy-start | bytes 100
  59.4 34.9 %all-to-all-start.1 = ((bf16[128,8,768]{0,2,1:T(8,128)(2,1)}), bf16[128,8,768]{0,2,1:T(8,128)(2,1)S(1)}, u32[]{:S(2)}, u32[]{:S(2)}) async-start(bf16[128,8,768]{0,2,1:T(8,128)(2,1)} %bitcast.83), calls=%async_computation.1 | async-start | bytes 3145728 | tf_op jit(solution)/shard_map/all_to_all | solution.py:42
  63.2 103.9 %reduce-scatter.3.cloned.1.call-start = ((), (), s32[]{:S(2)}) async-start(), calls=%async_computation.5 | async-start | bytes 7077888 | tf_op jit(solution)/shard_map/reduce_scatter | solution.py:56
  107.3 0.7 copy-start.1
  107.3 106.4 %reduce-scatter.5.cloned.1.call-start = ((), (), s32[]{:S(2)}) async-start(), calls=%async_computation.6 | async-start | bytes 1966080 | tf_op jit(solution)/shard_map/reduce_scatter | solution.py:94
  168.6 1.0 copy-start.5
  168.7 1.0 copy-start.6
  178.3 1.0 copy-start
  180.6 16.1 %all-to-all-start = ((bf16[8,32,1536]{2,1,0:T(8,128)(2,1)}), bf16[8,32,1536]{2,1,0:T(8,128)(2,1)S(1)}, u32[]{:S(2)}, u32[]{:S(2)}) async-start(bf16[8,32,1536]{2,1,0:T(8,128)(2,1)} %bitcast.3), calls=%async_computation | async-start | bytes 1572864 | tf_op jit(solution)/shard_map/all_to_all | solution.py:63
Sparse Core Ops, SparseCore 0:
  24.1 35.2 all-gather.3
  107.4 59.6 reduce-scatter.2
  178.4 35.2 reduce-scatter.4
where the time goes:
time: 221 us; the launch traced here: 220 us
  waiting for transfers between devices  123 us (56%)
  blocking collectives  37.5 us (17%)
  matrix products  23.2 us (10%)
  between operations  13.9 us (6%)
  local copies, waits for them, and re-layouts  12.6 us (6%)
  starting transfers between devices  7.45 us (3%)
  other arithmetic  2.56 us (1%)
    reduce_scatter x1, waiting for transfers between devices, on_device(): lax.psum_scatter(partial, 'dp', scatter_dimension=0, tiled=True)  59.1 us
    all_gather x1, waiting for transfers between devices, on_device(): wide = lax.all_gather(normed, 'mp', axis=1, tiled=True)  35.5 us
    all_gather x1, blocking collectives, on_device(): tables = lax.all_gather(tables, 'dp', axis=0, tiled=True)  24 us
    reduce_scatter x1, waiting for transfers between devices, on_device(): lax.psum_scatter(partial_value.astype(jnp.bfloat16), 'mp', scatter_dimens...  16 us
    psum x1, blocking collectives, on_device(): sums = lax.psum(sums, 'mp') / (feat_local * mp_count)  13.5 us
    all_to_all x1, waiting for transfers between devices, on_device(): lax.all_to_all(outgoing.reshape(pack_count, capacity, feat_local), 'dp',...  12.4 us
    dot_general x1, matrix products, on_device(): jnp.dot(ordered, qkv_weight.reshape(qkv_weight.shape[0], local_cols), pre...  12.2 us
    unnamed x18, local copies, waits for them, and re-layouts  10.7 us
  transfers between devices with their start and end apart: 5, of which 4 were waited for; matrix products, arithmetic and copies ran while one was open for 4% of the time, Pallas kernels for 0%

commit v1 on v0

--- a/solution.py
+++ b/solution.py
@@ -4,6 +4,23 @@
 from jax.sharding import PartitionSpec as P
 
 epsilon = 1e-06
+
+
+def joined_along(blocks, dim):
+    lengths = list(blocks.shape[1:])
+    lengths[dim] *= blocks.shape[0]
+    return jnp.moveaxis(blocks, 0, dim).reshape(lengths)
+
+
+def grow_blocks(x, axis):
+    count, index = (lax.axis_size(axis), lax.axis_index(axis))
+    parts, stride = (x[None], 1)
+    while stride < count:
+        other = lax.ppermute(parts, axis, [(i, i ^ stride) for i in range(count)])
+        low = index & stride == 0
+        parts = jnp.concatenate([jnp.where(low, parts, other), jnp.where(low, other, parts)])
+        stride *= 2
+    return parts
 
 
 def row_norm(values, scales):
@@ -41,7 +58,7 @@
     wide = lax.all_gather(normed, "mp", axis=1, tiled=True)
     slices = lax.all_to_all(wide, "dp", split_axis=1, concat_axis=0, tiled=True)
     tables = jnp.concatenate([send_start, run_length, slot_start], axis=0)[None]
-    tables = lax.all_gather(tables, "dp", axis=0, tiled=True)
+    tables = joined_along(grow_blocks(tables, "dp"), 0)
     starts, lengths, slots = (tables[:, 0].T, tables[:, 1].T, tables[:, 2])
     inside = (rows >= slots[:, :, None]) & (rows < (slots + lengths)[:, :, None])
     base = jnp.arange(pack_count, dtype=jnp.int32)[None, :] * pack_rows + starts - slots

time: 221 us -> 218 us (0.986)
  blocking collectives: 37.5 us -> 13.5 us
  waiting for transfers between devices: 123 us -> 140 us
  starting transfers between devices: 7.45 us -> 11 us
    all_gather x1 -> x0, blocking collectives: 24 us -> none  [on_device(): tables = lax.all_gather(tables, 'dp', axis=0, tiled=True)]
    ppermute x0 -> x3, waiting for transfers between devices: none -> 19.3 us  [grow_blocks(): other = lax.ppermute(parts, axis, [(i, i ^ stride) for i in range(count)])]
    ppermute x0 -> x3, starting transfers between devices: none -> 3.64 us  [grow_blocks(): other = lax.ppermute(parts, axis, [(i, i ^ stride) for i in range(count)])]
  transfers between devices with their start and end apart: 5 -> 8, of which waited for: 4 -> 6; matrix products, arithmetic and copies ran while one was open for 4% -> 5% of each run, Pallas kernels for 0% -> 0%
where the time goes in v1:
time: 218 us; the launch traced here: 217 us
  waiting for transfers between devices  140 us (64%)
  matrix products  23.2 us (11%)
  between operations  14 us (6%)
  blocking collectives  13.5 us (6%)
  local copies, waits for them, and re-layouts  12.6 us (6%)
  starting transfers between devices  11 us (5%)
  other arithmetic  2.6 us (1%)
    reduce_scatter x1, waiting for transfers between devices, on_device(): lax.psum_scatter(partial, 'dp', scatter_dimension=0, tiled=True)  58.2 us
    all_gather x1, waiting for transfers between devices, on_device(): wide = lax.all_gather(normed, 'mp', axis=1, tiled=True)  34.2 us
    ppermute x3, waiting for transfers between devices, grow_blocks(): other = lax.ppermute(parts, axis, [(i, i ^ stride) for i in range(count)])  19.3 us
    reduce_scatter x1, waiting for transfers between devices, on_device(): lax.psum_scatter(partial_value.astype(jnp.bfloat16), 'mp', scatter_dimens...  16 us
    psum x1, blocking collectives, on_device(): sums = lax.psum(sums, 'mp') / (feat_local * mp_count)  13.5 us
    all_to_all x1, waiting for transfers between devices, on_device(): lax.all_to_all(outgoing.reshape(pack_count, capacity, feat_local), 'dp',...  12.4 us
    dot_general x1, matrix products, on_device(): jnp.dot(ordered, qkv_weight.reshape(qkv_weight.shape[0], local_cols), pre...  12.2 us
    unnamed x18, local copies, waits for them, and re-layouts  10.7 us
  transfers between devices with their start and end apart: 8, of which 6 were waited for; matrix products, arithmetic and copies ran while one was open for 5% of the time, Pallas kernels for 0%

profile of v1, /device:TPU:0, one launch (start us, length us, event | category | flops | bytes accessed | tf_op | source)
XLA Modules:
  0.0 217.0 jit_solution(14200700429404013596)
XLA Ops:
  7.2 1.2 copy.33
  8.5 0.2 convert_reduce_fusion
  8.7 13.5 %psum.7 = f32[2,128]{1,0:T(2,128)S(1)} all-reduce(f32[2,128]{1,0:T(2,128)S(1)} %pad_maximum_fusion), channel_id=1, replica_groups=mesh['dp'=8,'mp'=4] {'mp'}, use_global_device_ids=true, to_apply=%region_3.4 | all-reduce | flops 256 | bytes 2048 | tf_op jit(solution)/shard_map/psum | solution.py:53
  22.2 0.8 dynamic_slice.3
  23.0 1.0 fusion.8
  24.1 1.1 collective-permute-done
  25.3 34.2 %all-gather.2.cloned.1.call-done = bf16[128,6144]{0,1:T(8,128)(2,1)} async-done(((bf16[128,1536]{0,1:T(8,128)(2,1)}), bf16[128,6144]{0,1:T(8,128)(2,1)}) %all-gather.2.cloned.1.call-update) | async-done | bytes 1572880 | tf_op jit(solution)/shard_map/all_gather | solution.py:58
  59.5 3.7 %all-to-all-start.1 = ((bf16[128,8,768]{0,2,1:T(8,128)(2,1)}), bf16[128,8,768]{0,2,1:T(8,128)(2,1)S(1)}, u32[]{:S(2)}, u32[]{:S(2)}) async-start(bf16[128,8,768]{0,2,1:T(8,128)(2,1)} %bitcast.83), calls=%async_computation.1 | async-start | bytes 3145728 | tf_op jit(solution)/shard_map/all_to_all | solution.py:59
  63.2 2.0 collective-permute-start.1
  65.2 18.1 %collective-permute-done.1 = s32[2,1,3,8]{3,2,1,0:T(4,128)S(1)} collective-permute-done((s32[2,1,3,8]{3,2,1,0:T(4,128)S(1)}, s32[2,1,3,8]{3,2,1,0:T(4,128)S(1)}, u32[]{:S(2)}, u32[]{:S(2)}) %collective-permute-start.1) | collective-permute-done | bytes 224 | tf_op jit(solution)/shard_map/ppermute | solution.py:19
  83.4 1.5 collective-permute-start.2
  84.9 6.7 %copy.35 = bf16[768,3,1024]{0,2,1:T(8,128)(2,1)} copy(bf16[768,3,1024]{2,0,1:T(8,128)(2,1)} %param.16) | data formatting | bytes 9437184 | tf_op args[6]
  91.8 0.1 select_reduce_fusion
  91.9 0.7 copy.34
  92.6 12.2 %convolution_convert_fusion.1 = bf16[1024,3072]{1,0:T(8,128)(2,1)} fusion(bf16[768,3072]{0,1:T(8,128)(2,1)} %bitcast.79, bf16[1024,768]{1,0:T(8,128)(2,1)S(1)} %bitcast.84, s32[1024]{0:T(1024)S(1)} %bitcast.93), kind=kOutput, calls=%fused_computation.1 | convolution fusion | flops 6447431680 | bytes 12587008 | tf_op jit(solution)/shard_map/dot_general | solution.py:68
  104.9 0.6 copy-done.3
  105.6 58.2 %reduce-scatter.3.cloned.1.call-done = bf16[128,3072]{1,0:T(8,128)(2,1)} async-done(((bf16[1024,3072]{1,0:T(8,128)(2,1)}), bf16[128,3072]{1,0:T(8,128)(2,1)}) %reduce-scatter.3.cloned.1.call-update) | async-done | bytes 786448 | tf_op jit(solution)/shard_map/reduce_scatter | solution.py:73
  163.9 1.3 copy.41
  165.1 0.2 copy_convert_fusion
  165.4 0.3 slice_reduce_fusion.1
  165.7 0.3 fusion.16
  166.1 0.2 copy.40
  166.4 0.7 fusion.4
  167.1 0.3 convolution_convert_fusion.4
  167.4 7.6 %convolution_convert_fusion = bf16[128,6144]{1,0:T(8,128)(2,1)} fusion(bf16[128,1024]{0,1:T(8,128)(2,1)S(1)} %bitcast.86, bf16[1024,6144]{1,0:T(8,128)(2,1)} %param.19), kind=kOutput, calls=%fused_computation | convolution fusion | flops 1611399168 | bytes 14417920 | tf_op jit(solution)/shard_map/dot_general | solution.py:110
  175.2 0.1 lt.37
  175.3 0.7 copy-done
  176.0 1.3 convolution_convert_fusion.2
  177.3 3.5 %all-to-all-start = ((bf16[8,32,1536]{2,1,0:T(8,128)(2,1)}), bf16[8,32,1536]{2,1,0:T(8,128)(2,1)S(1)}, u32[]{:S(2)}, u32[]{:S(2)}) async-start(bf16[8,32,1536]{2,1,0:T(8,128)(2,1)} %bitcast.3), calls=%async_computation | async-start | bytes 1572864 | tf_op jit(solution)/shard_map/all_to_all | solution.py:80
  181.0 12.4 %all-to-all-done = bf16[8,32,1536]{2,1,0:T(8,128)(2,1)S(1)} async-done(((bf16[8,32,1536]{2,1,0:T(8,128)(2,1)}), bf16[8,32,1536]{2,1,0:T(8,128)(2,1)S(1)}, u32[]{:S(2)}, u32[]{:S(2)}) %all-to-all-start) | async-done | bytes 786464 | tf_op jit(solution)/shard_map/all_to_all | solution.py:80
  193.4 1.0 convolution_convert_fusion.3
  194.4 16.0 %reduce-scatter.5.cloned.1.call-done = bf16[128,1536]{1,0:T(8,128)(2,1)} async-done(((bf16[128,6144]{1,0:T(8,128)(2,1)}), bf16[128,1536]{1,0:T(8,128)(2,1)}) %reduce-scatter.5.cloned.1.call-update) | async-done | bytes 393232 | tf_op jit(solution)/shard_map/reduce_scatter | solution.py:111
  (45 shorter events, 1.0 us)
Async XLA Ops:
  7.2 16.8 %copy-start.1 = (s32[1,8]{1,0:T(1,128)S(1)}, s32[1,8]{1,0:T(1,128)}, u32[]{:S(2)}) copy-start(s32[1,8]{1,0:T(1,128)} %param.11) | copy-start | bytes 100
  7.2 16.8 %copy-start.4 = (s32[1,8]{1,0:T(1,128)S(1)}, s32[1,8]{1,0:T(1,128)}, u32[]{:S(2)}) copy-start(s32[1,8]{1,0:T(1,128)} %param.12) | copy-start | bytes 100
  7.2 16.8 %copy-start.2 = (s32[1,8]{1,0:T(1,128)S(1)}, s32[1,8]{1,0:T(1,128)}, u32[]{:S(2)}) copy-start(s32[1,8]{1,0:T(1,128)} %param.13) | copy-start | bytes 100
  7.2 52.3 %all-gather.2.cloned.1.call-start = ((), (), s32[]{:S(2)}) async-start(), calls=%async_computation.4 | async-start | bytes 1966080 | tf_op jit(solution)/shard_map/all_gather | solution.py:58
  24.1 1.2 collective-permute-start
  59.5 32.4 %all-to-all-start.1 = ((bf16[128,8,768]{0,2,1:T(8,128)(2,1)}), bf16[128,8,768]{0,2,1:T(8,128)(2,1)S(1)}, u32[]{:S(2)}, u32[]{:S(2)}) async-start(bf16[128,8,768]{0,2,1:T(8,128)(2,1)} %bitcast.83), calls=%async_computation.1 | async-start | bytes 3145728 | tf_op jit(solution)/shard_map/all_to_all | solution.py:59
  63.1 100.7 %reduce-scatter.3.cloned.1.call-start = ((), (), s32[]{:S(2)}) async-start(), calls=%async_computation.5 | async-start | bytes 7077888 | tf_op jit(solution)/shard_map/reduce_scatter | solution.py:73
  63.2 20.2 %collective-permute-start.1 = (s32[2,1,3,8]{3,2,1,0:T(4,128)S(1)}, s32[2,1,3,8]{3,2,1,0:T(4,128)S(1)}, u32[]{:S(2)}, u32[]{:S(2)}) collective-permute-start(s32[2,1,3,8]{3,2,1,0:T(4,128)S(1)} %pad_add_fusion.1), channel_id=1, source_target_pairs={{0,8},{4,12},{8,0},{12,4},{16,24},{20,28},{24,16},{28,20},{1,9},{5... | collective-permute-start | bytes 584 | tf_op jit(solution)/shard_map/ppermute | solution.py:19
  83.4 8.3 %collective-permute-start.2 = (s32[4,1,3,8]{3,2,1,0:T(4,128)S(1)}, s32[4,1,3,8]{3,2,1,0:T(4,128)S(1)}, u32[]{:S(2)}, u32[]{:S(2)}) collective-permute-start(s32[4,1,3,8]{3,2,1,0:T(4,128)S(1)} %pad_add_fusion), channel_id=1, source_target_pairs={{0,16},{4,20},{8,24},{12,28},{16,0},{20,4},{24,8},{28,12},{1,17},{... | collective-permute-start | bytes 1160 | tf_op jit(solution)/shard_map/ppermute | solution.py:19
  104.9 0.7 copy-start.3
  104.9 105.5 %reduce-scatter.5.cloned.1.call-start = ((), (), s32[]{:S(2)}) async-start(), calls=%async_computation.6 | async-start | bytes 1966080 | tf_op jit(solution)/shard_map/reduce_scatter | solution.py:111
  165.3 1.0 copy-start.5
  165.3 1.0 copy-start.6
  175.0 1.0 copy-start
  177.3 16.1 %all-to-all-start = ((bf16[8,32,1536]{2,1,0:T(8,128)(2,1)}), bf16[8,32,1536]{2,1,0:T(8,128)(2,1)S(1)}, u32[]{:S(2)}, u32[]{:S(2)}) async-start(bf16[8,32,1536]{2,1,0:T(8,128)(2,1)} %bitcast.3), calls=%async_computation | async-start | bytes 1572864 | tf_op jit(solution)/shard_map/all_to_all | solution.py:80
Sparse Core Ops, SparseCore 0:
  24.1 35.2 all-gather.1
  105.0 58.7 reduce-scatter.2
  175.1 35.2 reduce-scatter.4
